TPU v7x, 32 devices: a whole 2x2x4 slice. The times are simulated.
32 devices in a mesh: leaf: 4 (over y, core), panel: 8 (over z, x).
Axes of the slice: x: 2, y: 2, z: 4, core: 2. Of those that a mesh axis runs over, the one named last changes fastest.
Arguments:
- pivot_rhs: float32 [4, 48, 4096], P('leaf', None, 'panel'), may hold values from -6 to 6
- subtree_update: float32 [4, 64, 4096], P('leaf', None, 'panel'), may hold values from -6 to 6
- lower_pivot: bfloat16 [2, 4, 4096, 4096], P(None, 'leaf', 'panel'), as said below
- lower_update: bfloat16 [2, 4, 4096, 4096], P(None, 'leaf', None, 'panel'), as said below
- row_map: int32 [2, 4, 2, 4096], P(None, 'leaf', None, 'panel'), may hold values from 0 to 1023, as said below
- root_inverse: bfloat16 [4096, 4096], P('panel'), as said below
Outputs:
- pivot_solution: float32 [4, 48, 4096], P('leaf', None, 'panel')
- subtree_solution: float32 [4, 64, 4096], P('leaf', None, 'panel')
Inputs may be any that keep to these rules, and one draw needn't show every extreme that they name: row_map[l, i] is the same for all i that share i >> (l + 1); within one panel block of 512 rows of one child the values are distinct. lower_pivot[l, i] is the same for all i that share i >> (l + 1), and is zero above its diagonal blocks of 512 rows. lower_update[l, i] is the same for all i that share i >> (l + 1). root_inverse is symmetric.
All inputs are finite; a program needn't handle non-finite values.
Results may differ from a plain program's by a relative error of at most 0.0003.
Values sent between devices are 32-bit elements; how exact they have to be, the bound alone decides.
A program may use at most 64 MiB of HBM per device.

v0:
```python
import jax
import jax.numpy as jnp
from jax import lax
from jax.sharding import PartitionSpec as P

HIGHEST_PRECISION = lax.Precision.HIGHEST
CONTRACT_LAST = (((1,), (1,)), ((), ()))
CONTRACT_FIRST_LAST = (((0,), (1,)), ((), ()))


def partner(value, axis, stride):
    return lax.ppermute(value, axis, [(i, i ^ 1 << stride) for i in range(lax.axis_size(axis))])


def local(pivot_rhs, subtree_update, lower_pivot, lower_update, row_map, root_inverse):
    levels = lax.axis_size("leaf").bit_length() - 1
    leaf_index = lax.axis_index("leaf")
    pivot_block = pivot_rhs.shape[2]
    update_block = subtree_update.shape[2]
    slot_count = pivot_block + update_block
    current = subtree_update[0]
    solved_levels = []
    onehot_tables = []
    leaf_bits = []
    offset = 0
    for tree_level in range(levels):
        leaf_bit = leaf_index >> tree_level & 1
        col_count = current.shape[0] // 2
        halves = current.reshape(col_count, 2, update_block)
        kept_half = jnp.where(leaf_bit == 0, halves[:, 0], halves[:, 1])
        sent_half = jnp.where(leaf_bit == 0, halves[:, 1], halves[:, 0])
        received = partner(sent_half, "leaf", tree_level)
        children = jnp.where(
            leaf_bit == 0,
            jnp.concatenate([kept_half, received], 1),
            jnp.concatenate([received, kept_half], 1),
        )
        maps = row_map[tree_level, 0].reshape(2 * update_block)
        onehot_table = (maps[:, None] == jnp.arange(slot_count, dtype=jnp.int32)[None, :]).astype(
            jnp.float32
        )
        assembled = jnp.dot(children, onehot_table, precision=HIGHEST_PRECISION)
        right_side = pivot_rhs[0, offset : offset + col_count] + assembled[:, :pivot_block]
        offset = offset + col_count
        inverse_rows = lower_pivot[tree_level, 0]
        update_cols = lower_update[tree_level, 0]
        inverse_cols = inverse_rows.astype(jnp.float32)
        solved = lax.dot_general(
            lax.all_gather(right_side, "panel", axis=1, tiled=True),
            inverse_cols,
            CONTRACT_LAST,
            precision=HIGHEST_PRECISION,
        )
        factor_rows = update_cols.astype(jnp.float32)
        coupled_update = lax.psum_scatter(
            lax.dot_general(factor_rows, solved, CONTRACT_LAST, precision=HIGHEST_PRECISION),
            "panel",
            scatter_dimension=0,
            tiled=True,
        ).T
        current = assembled[:, pivot_block:] - coupled_update
        solved_levels.append(solved)
        onehot_tables.append(onehot_table)
        leaf_bits.append(leaf_bit)
    root_inverse_cols = root_inverse.astype(jnp.float32)
    known = lax.dot_general(
        lax.all_gather(current, "panel", axis=1, tiled=True),
        root_inverse_cols,
        CONTRACT_LAST,
        precision=HIGHEST_PRECISION,
    )
    pieces = [None] * levels
    for tree_level in range(levels - 1, -1, -1):
        inverse_rows = lower_pivot[tree_level, 0]
        update_cols = lower_update[tree_level, 0]
        forward_part = solved_levels[tree_level]
        col_count = forward_part.shape[0]
        known_factor_rows = update_cols.astype(jnp.float32)
        coupling = jnp.dot(
            lax.all_gather(known, "panel", axis=1, tiled=True),
            known_factor_rows,
            precision=HIGHEST_PRECISION,
        )
        residual_part = forward_part - coupling
        pivot_inverse_cols = inverse_rows.astype(jnp.float32)
        own_x = lax.psum_scatter(
            lax.dot_general(
                pivot_inverse_cols, residual_part, CONTRACT_FIRST_LAST, precision=HIGHEST_PRECISION
            ),
            "panel",
            scatter_dimension=0,
            tiled=True,
        ).T
        pieces[tree_level] = own_x
        whole_front = jnp.concatenate([own_x, known], 1)
        children = lax.dot_general(
            whole_front, onehot_tables[tree_level], CONTRACT_LAST, precision=HIGHEST_PRECISION
        )
        leaf_bit = leaf_bits[tree_level]
        first_child = children[:, :update_block]
        second_child = children[:, update_block:]
        own_child = jnp.where(leaf_bit == 0, first_child, second_child)
        sent_child = jnp.where(leaf_bit == 0, second_child, first_child)
        received = partner(sent_child, "leaf", tree_level)
        paired = jnp.where(
            leaf_bit == 0, jnp.stack([own_child, received], 1), jnp.stack([received, own_child], 1)
        )
        known = paired.reshape(2 * col_count, update_block)
    return (jnp.concatenate(pieces, 0)[None], known[None])


def solution(mesh):
    in_specs = (
        P("leaf", None, "panel"),
        P("leaf", None, "panel"),
        P(None, "leaf", "panel", None),
        P(None, "leaf", None, "panel"),
        P(None, "leaf", None, "panel"),
        P("panel", None),
    )
    out_specs = (P("leaf", None, "panel"), P("leaf", None, "panel"))
    return jax.shard_map(local, mesh=mesh, in_specs=in_specs, out_specs=out_specs, check_vma=False)
```

profile of v0, /device:TPU:1, one launch (start us, length us, event | category | flops | bytes accessed | tf_op | source)
XLA Modules:
  0.0 490.3 jit_solution(4684953163303562873)
XLA Ops:
  7.2 0.0 reduce-scatter.5.cloned.1.call-start
  7.2 1.0 reshape_squeeze.3
  8.2 0.1 fusion.58
  8.3 0.1 collective-permute-start
  8.5 0.7 slice_bitcast_fusion.1
  9.2 0.5 collective-permute-done
  9.7 1.6 fusion.15
  11.3 0.9 slice_add_fusion
  12.2 26.9 %all_gather.15 = f32[32,4096]{1,0:T(8,128)S(1)} all-gather(f32[32,512]{1,0:T(8,128)S(1)} %slice_add_fusion), channel_id=1, replica_groups=mesh['leaf'=4,'panel'=8] {'panel'}, dimensions={1}, use_global_device_ids=true | all-gather | bytes 589824 | tf_op jit(solution)/shard_map/all_gather | solution.py:49
  39.0 5.9 %fusion.10 = f32[32,512]{1,0:T(8,128)S(1)} fusion(f32[32,4096]{1,0:T(8,128)S(1)} %all_gather.15, bf16[2,1,512,4096]{3,2,1,0:T(8,128)(2,1)} %param.8), kind=kOutput, calls=%fused_computation.14 | convolution fusion | flops 805306368 | bytes 4784128 | tf_op jit(solution)/shard_map/dot_general | solution.py:48
  44.9 6.7 %convolution_bitcast_fusion.1 = f32[4096,32]{0,1:T(8,128)} fusion(f32[32,512]{1,0:T(8,128)S(1)} %fusion.10, bf16[2,1,4096,512]{3,2,1,0:T(8,128)(2,1)} %param.9), kind=kOutput, calls=%fused_computation.1 | convolution fusion | flops 805306368 | bytes 4784128 | tf_op jit(solution)/shard_map/dot_general | solution.py:56
  51.6 0.0 reduce-scatter.5.cloned.1.call-update
  51.6 0.0 reduce-scatter.7.cloned.1.call-start
  51.7 67.1 %reduce-scatter.5.cloned.1.call-done = f32[512,32]{0,1:T(8,128)} async-done(((f32[4096,32]{0,1:T(8,128)}), f32[512,32]{0,1:T(8,128)}) %reduce-scatter.5.cloned.1.call-update) | async-done | bytes 65552 | tf_op jit(solution)/shard_map/reduce_scatter | solution.py:55
  118.8 0.8 slice_subtract_fusion
  119.7 0.1 fusion.59
  119.8 1.3 collective-permute-start.1
  121.1 1.5 collective-permute-done.1
  122.6 1.5 fusion.13
  124.1 0.8 slice_add_fusion.1
  124.8 24.7 %all_gather.16 = f32[16,4096]{1,0:T(8,128)S(1)} all-gather(f32[16,512]{1,0:T(8,128)S(1)} %slice_add_fusion.1), channel_id=1, replica_groups=mesh['leaf'=4,'panel'=8] {'panel'}, dimensions={1}, use_global_device_ids=true | all-gather | bytes 294912 | tf_op jit(solution)/shard_map/all_gather | solution.py:49
  149.6 5.5 %fusion.4 = f32[16,512]{1,0:T(8,128)S(1)} fusion(f32[16,4096]{1,0:T(8,128)S(1)} %all_gather.16, bf16[2,1,512,4096]{3,2,1,0:T(8,128)(2,1)} %param.8), kind=kOutput, calls=%fused_computation.8 | convolution fusion | flops 402653184 | bytes 4489216 | tf_op jit(solution)/shard_map/dot_general | solution.py:48
  155.1 6.3 %convolution_bitcast_fusion.3 = f32[4096,16]{0,1:T(8,128)} fusion(f32[16,512]{1,0:T(8,128)S(1)} %fusion.4, bf16[2,1,4096,512]{3,2,1,0:T(8,128)(2,1)} %param.9), kind=kOutput, calls=%fused_computation.3 | convolution fusion | flops 402653184 | bytes 4489216 | tf_op jit(solution)/shard_map/dot_general | solution.py:56
  161.4 0.0 reduce-scatter.7.cloned.1.call-update
  161.4 0.0 reduce-scatter.9.cloned.1.call-start
  161.5 67.8 %reduce-scatter.7.cloned.1.call-done = f32[512,16]{0,1:T(8,128)} async-done(((f32[4096,16]{0,1:T(8,128)}), f32[512,16]{0,1:T(8,128)}) %reduce-scatter.7.cloned.1.call-update) | async-done | bytes 32784 | tf_op jit(solution)/shard_map/reduce_scatter | solution.py:55
  229.3 0.8 slice_subtract_fusion.1
  230.1 25.2 %all_gather.17 = f32[16,4096]{1,0:T(8,128)S(1)} all-gather(f32[16,512]{1,0:T(8,128)S(1)} %slice_subtract_fusion.1), channel_id=1, replica_groups=mesh['leaf'=4,'panel'=8] {'panel'}, dimensions={1}, use_global_device_ids=true | all-gather | bytes 294912 | tf_op jit(solution)/shard_map/all_gather | solution.py:67
  255.2 5.5 %fusion.60 = f32[16,512]{1,0:T(8,128)S(1)} fusion(f32[16,4096]{1,0:T(8,128)S(1)} %all_gather.17, bf16[512,4096]{1,0:T(8,128)(2,1)} %param.11), kind=kOutput, calls=%fused_computation.83 | convolution fusion | flops 402653184 | bytes 4489216 | tf_op jit(solution)/shard_map/dot_general | solution.py:66
  260.7 24.4 %all_gather.18 = f32[16,4096]{1,0:T(8,128)S(1)} all-gather(f32[16,512]{1,0:T(8,128)S(1)} %fusion.60), channel_id=1, replica_groups=mesh['leaf'=4,'panel'=8] {'panel'}, dimensions={1}, use_global_device_ids=true | all-gather | bytes 294912 | tf_op jit(solution)/shard_map/all_gather | solution.py:80
  285.2 3.9 fusion.31
  289.1 4.7 convolution_bitcast_fusion.2
  293.8 0.0 reduce-scatter.9.cloned.1.call-update
  293.8 0.0 reduce-scatter.11.cloned.1.call-start
  293.8 72.5 %reduce-scatter.9.cloned.1.call-done = f32[512,16]{0,1:T(8,128)} async-done(((f32[4096,16]{0,1:T(8,128)}), f32[512,16]{0,1:T(8,128)}) %reduce-scatter.9.cloned.1.call-update) | async-done | bytes 32784 | tf_op jit(solution)/shard_map/reduce_scatter | solution.py:86
  366.3 2.8 fusion.12
  369.1 1.3 collective-permute-start.2
  370.4 1.6 collective-permute-done.2
  371.9 0.1 copy.24
  372.1 25.7 %all_gather.19 = f32[32,4096]{1,0:T(8,128)S(1)} all-gather(f32[32,512]{1,0:T(8,128)S(1)} %select_n.121), channel_id=1, replica_groups=mesh['leaf'=4,'panel'=8] {'panel'}, dimensions={1}, use_global_device_ids=true | all-gather | bytes 589824 | tf_op jit(solution)/shard_map/all_gather | solution.py:80
  397.7 4.3 fusion.28
  402.0 0.0 copy-start
  402.0 5.1 %convolution_bitcast_fusion = f32[4096,32]{0,1:T(8,128)} fusion(f32[32,512]{1,0:T(8,128)S(1)} %fusion.28, bf16[2,1,512,4096]{3,2,1,0:T(8,128)(2,1)} %param.8), kind=kOutput, calls=%fused_computation | convolution fusion | flops 805306368 | bytes 4784128 | tf_op jit(solution)/shard_map/dot_general | solution.py:87
  407.2 0.0 reduce-scatter.11.cloned.1.call-update
  407.2 68.5 %reduce-scatter.11.cloned.1.call-done = f32[512,32]{0,1:T(8,128)} async-done(((f32[4096,32]{0,1:T(8,128)}), f32[512,32]{0,1:T(8,128)}) %reduce-scatter.11.cloned.1.call-update) | async-done | bytes 65552 | tf_op jit(solution)/shard_map/reduce_scatter | solution.py:86
  475.7 3.0 fusion.14
  478.7 2.6 collective-permute-start.3
  481.4 0.0 copy-done
  481.4 1.5 maximum_bitcast_fusion
  482.9 0.0 collective-permute-done.3
  482.9 0.1 copy.25
  483.0 0.7 select_n.127
  (12 shorter events, 0.2 us)
Async XLA Ops:
  7.2 111.6 %reduce-scatter.5.cloned.1.call-start = ((), (), s32[]{:S(2)}) async-start(), calls=%async_computation.4 | async-start | bytes 589824 | tf_op jit(solution)/shard_map/reduce_scatter | solution.py:55
  8.3 1.3 collective-permute-start
  51.6 177.7 %reduce-scatter.7.cloned.1.call-start = ((), (), s32[]{:S(2)}) async-start(), calls=%async_computation.5 | async-start | bytes 294912 | tf_op jit(solution)/shard_map/reduce_scatter | solution.py:55
  119.8 2.8 collective-permute-start.1
  161.4 204.9 %reduce-scatter.9.cloned.1.call-start = ((), (), s32[]{:S(2)}) async-start(), calls=%async_computation.6 | async-start | bytes 294912 | tf_op jit(solution)/shard_map/reduce_scatter | solution.py:86
  293.8 181.9 %reduce-scatter.11.cloned.1.call-start = ((), (), s32[]{:S(2)}) async-start(), calls=%async_computation.7 | async-start | bytes 589824 | tf_op jit(solution)/shard_map/reduce_scatter | solution.py:86
  369.1 2.8 collective-permute-start.2
  402.0 79.3 %copy-start = (f32[512,16]{0,1:T(8,128)S(1)}, f32[512,16]{0,1:T(8,128)}, u32[]{:S(2)}) copy-start(f32[512,16]{0,1:T(8,128)} %reduce-scatter.9.cloned.1.call-done) | copy-start | bytes 98308
  478.7 4.1 collective-permute-start.3
Sparse Core Ops, SparseCore 0:
  51.7 67.0 reduce-scatter.4
  161.5 67.7 reduce-scatter.6
  293.9 72.3 reduce-scatter.8
  407.3 68.3 reduce-scatter.10
where the time goes:
time: 491 us; the launch traced here: 490 us
  waiting for transfers between devices  280 us (57%)
  blocking collectives  127 us (26%)
  matrix products  56.8 us (12%)
  between operations  13.9 us (3%)
  starting transfers between devices  5.46 us (1%)
  other arithmetic  4.96 us (1%)
    reduce_scatter x2, waiting for transfers between devices, local(): lax.psum_scatter(lax.dot_general(pivot_inverse_cols, residual_part, CONTR...  141 us
    reduce_scatter x2, waiting for transfers between devices, local(): lax.psum_scatter(lax.dot_general(factor_rows, solved, CONTRACT_LAST, prec...  135 us
    all_gather x2, blocking collectives, local(): lax.all_gather(right_side, 'panel', axis=1, tiled=True)  51.6 us
    all_gather x2, blocking collectives, local(): lax.all_gather(known, 'panel', axis=1, tiled=True)  50.1 us
    all_gather x1, blocking collectives, local(): lax.all_gather(current, 'panel', axis=1, tiled=True)  25.2 us
    dot_general x2, matrix products, local(): lax.dot_general(factor_rows, solved, CONTRACT_LAST, precision=HIGHEST_PRE...  12.9 us
    dot_general x2, matrix products, local(): lax.dot_general(lax.all_gather(right_side, 'panel', axis=1, tiled=True),...  11.4 us
  transfers between devices with their start and end apart: 8, of which 7 were waited for; matrix products, arithmetic and copies ran while one was open for 0% of the time, Pallas kernels for 0%

commit v1 on v0

--- a/solution.py
+++ b/solution.py
@@ -6,6 +6,18 @@
 HIGHEST_PRECISION = lax.Precision.HIGHEST
 CONTRACT_LAST = (((1,), (1,)), ((), ()))
 CONTRACT_FIRST_LAST = (((0,), (1,)), ((), ()))
+
+
+def collect(shard, axis, dim):
+    ways, here, step = (lax.axis_size(axis), lax.axis_index(axis), shard.shape[dim])
+    line, have = (shard, 1)
+    while have < ways:
+        line = jnp.concatenate(
+            [line, lax.ppermute(line, axis, [(d, (d - have) % ways) for d in range(ways)])],
+            axis=dim,
+        )
+        have = 2 * have
+    return jnp.roll(line, here * step, axis=dim)
 
 
 def partner(value, axis, stride):
@@ -46,7 +58,7 @@
         update_cols = lower_update[tree_level, 0]
         inverse_cols = inverse_rows.astype(jnp.float32)
         solved = lax.dot_general(
-            lax.all_gather(right_side, "panel", axis=1, tiled=True),
+            collect(right_side, "panel", 1),
             inverse_cols,
             CONTRACT_LAST,
             precision=HIGHEST_PRECISION,

time: 491 us -> 473 us (0.963)
  blocking collectives: 127 us -> 75.3 us
  waiting for transfers between devices: 280 us -> 301 us
  starting transfers between devices: 5.46 us -> 16.5 us
    all_gather x2 -> x0, blocking collectives: 51.6 us -> none  [local(): lax.all_gather(right_side, 'panel', axis=1, tiled=True)]
    ppermute x0 -> x6, waiting for transfers between devices: none -> 27 us  [collect(): lax.ppermute(line, axis, [(d, (d - have) % ways) for d in range(ways)])]
    ppermute x0 -> x6, starting transfers between devices: none -> 11 us  [collect(): lax.ppermute(line, axis, [(d, (d - have) % ways) for d in range(ways)])]
    reduce_scatter x2, waiting for transfers between devices: 135 us -> 130 us  [local(): lax.psum_scatter(lax.dot_general(factor_rows, solved, CONTRACT_LAST, prec...]
  transfers between devices with their start and end apart: 8 -> 14, of which waited for: 7 -> 13; matrix products, arithmetic and copies ran while one was open for 0% -> 0% of each run, Pallas kernels for 0% -> 0%
where the time goes in v1:
time: 473 us; the launch traced here: 472 us
  waiting for transfers between devices  301 us (64%)
  blocking collectives  75.3 us (16%)
  matrix products  56.8 us (12%)
  starting transfers between devices  16.5 us (3%)
  between operations  14.1 us (3%)
  other arithmetic  5 us (1%)
    reduce_scatter x2, waiting for transfers between devices, local(): lax.psum_scatter(lax.dot_general(pivot_inverse_cols, residual_part, CONTR...  141 us
    reduce_scatter x2, waiting for transfers between devices, local(): lax.psum_scatter(lax.dot_general(factor_rows, solved, CONTRACT_LAST, prec...  130 us
    all_gather x2, blocking collectives, local(): lax.all_gather(known, 'panel', axis=1, tiled=True)  50.2 us
    ppermute x6, waiting for transfers between devices, collect(): lax.ppermute(line, axis, [(d, (d - have) % ways) for d in range(ways)])  27 us
    all_gather x1, blocking collectives, local(): lax.all_gather(current, 'panel', axis=1, tiled=True)  25.1 us
    dot_general x2, matrix products, local(): lax.dot_general(factor_rows, solved, CONTRACT_LAST, precision=HIGHEST_PRE...  12.9 us
    dot_general x2, matrix products, local(): lax.dot_general(collect(right_side, 'panel', 1), inverse_cols, CONTRACT_L...  11.4 us
    ppermute x6, starting transfers between devices, collect(): lax.ppermute(line, axis, [(d, (d - have) % ways) for d in range(ways)])  11 us
  transfers between devices with their start and end apart: 14, of which 13 were waited for; matrix products, arithmetic and copies ran while one was open for 0% of the time, Pallas kernels for 0%

profile of v1, /device:TPU:1, one launch (start us, length us, event | category | flops | bytes accessed | tf_op | source)
XLA Modules:
  0.0 471.9 jit_solution(6415908847836129126)
XLA Ops:
  7.2 0.0 reduce-scatter.5.cloned.1.call-start
  7.2 1.0 reshape_squeeze.3
  8.2 0.1 fusion.62
  8.3 0.1 collective-permute-start
  8.5 0.7 slice_bitcast_fusion.1
  9.2 0.5 collective-permute-done
  9.7 1.6 fusion.15
  11.3 0.9 constant_dynamic-update-slice_fusion.7
  12.2 5.5 %collective-permute-start.1 = (f32[32,512]{1,0:T(8,128)S(1)}, f32[32,512]{1,0:T(8,128)S(1)}, u32[]{:S(2)}, u32[]{:S(2)}) collective-permute-start(f32[32,512]{1,0:T(8,128)S(1)} %get-tuple-element.5), channel_id=1, source_target_pairs={{0,7},{1,0},{2,1},{3,2},{4,3},{5,4},{6,5},{7,6},{8,15},{9,8},{10,9... | collective-permute-start | bytes 196616 | tf_op jit(solution)/shard_map/ppermute | solution.py:16
  17.6 1.3 collective-permute-done.1
  19.0 0.9 collective-permute-start.2
  19.9 3.0 collective-permute-done.2
  22.9 0.1 collective-permute-start.3
  23.0 14.3 %collective-permute-done.3 = f32[32,2048]{1,0:T(8,128)S(1)} collective-permute-done((f32[32,2048]{1,0:T(8,128)S(1)}, f32[32,2048]{1,0:T(8,128)S(1)}, u32[]{:S(2)}, u32[]{:S(2)}) %collective-permute-start.3) | collective-permute-done | bytes 262176 | tf_op jit(solution)/shard_map/ppermute | solution.py:16
  37.4 5.9 %fusion.10 = f32[32,512]{1,0:T(8,128)S(1)} fusion(bf16[2,1,512,4096]{3,2,1,0:T(8,128)(2,1)} %param.8, f32[32,8192]{1,0:T(8,128)S(1)} %constant_dynamic-update-slice_fusion, s32[]{:T(128)S(6)} %select_n.129), kind=kOutput, calls=%fused_computation.14 | convolution fusion | flops 805306368 | bytes 4784132 | tf_op jit(solution)/shard_map/dot_general | solution.py:60
  43.3 6.7 %convolution_bitcast_fusion.1 = f32[4096,32]{0,1:T(8,128)} fusion(f32[32,512]{1,0:T(8,128)S(1)} %fusion.10, bf16[2,1,4096,512]{3,2,1,0:T(8,128)(2,1)} %param.9), kind=kOutput, calls=%fused_computation.1 | convolution fusion | flops 805306368 | bytes 4784128 | tf_op jit(solution)/shard_map/dot_general | solution.py:68
  50.0 0.0 reduce-scatter.5.cloned.1.call-update
  50.0 0.0 reduce-scatter.7.cloned.1.call-start
  50.1 62.6 %reduce-scatter.5.cloned.1.call-done = f32[512,32]{0,1:T(8,128)} async-done(((f32[4096,32]{0,1:T(8,128)}), f32[512,32]{0,1:T(8,128)}) %reduce-scatter.5.cloned.1.call-update) | async-done | bytes 65552 | tf_op jit(solution)/shard_map/reduce_scatter | solution.py:67
  112.6 0.8 slice_subtract_fusion
  113.5 0.1 fusion.63
  113.6 1.2 collective-permute-start.4
  114.9 1.6 collective-permute-done.4
  116.4 1.5 fusion.13
  117.9 0.8 constant_dynamic-update-slice_fusion.15
  118.7 2.3 collective-permute-start.5
  121.0 1.0 collective-permute-done.5
  122.0 1.4 collective-permute-start.6
  123.4 1.7 collective-permute-done.6
  125.1 0.9 collective-permute-start.7
  126.1 5.6 %collective-permute-done.7 = f32[16,2048]{1,0:T(8,128)S(1)} collective-permute-done((f32[16,2048]{1,0:T(8,128)S(1)}, f32[16,2048]{1,0:T(8,128)S(1)}, u32[]{:S(2)}, u32[]{:S(2)}) %collective-permute-start.7) | collective-permute-done | bytes 131104 | tf_op jit(solution)/shard_map/ppermute | solution.py:16
  131.8 5.5 %fusion.4 = f32[16,512]{1,0:T(8,128)S(1)} fusion(bf16[2,1,512,4096]{3,2,1,0:T(8,128)(2,1)} %param.8, f32[16,8192]{1,0:T(8,128)S(1)} %constant_dynamic-update-slice_fusion.8, s32[]{:T(128)S(6)} %select_n.129), kind=kOutput, calls=%fused_computation.8 | convolution fusion | flops 402653184 | bytes 4489220 | tf_op jit(solution)/shard_map/dot_general | solution.py:60
  137.3 6.3 %convolution_bitcast_fusion.3 = f32[4096,16]{0,1:T(8,128)} fusion(f32[16,512]{1,0:T(8,128)S(1)} %fusion.4, bf16[2,1,4096,512]{3,2,1,0:T(8,128)(2,1)} %param.9), kind=kOutput, calls=%fused_computation.3 | convolution fusion | flops 402653184 | bytes 4489216 | tf_op jit(solution)/shard_map/dot_general | solution.py:68
  143.6 0.0 reduce-scatter.7.cloned.1.call-update
  143.6 0.0 reduce-scatter.9.cloned.1.call-start
  143.6 67.3 %reduce-scatter.7.cloned.1.call-done = f32[512,16]{0,1:T(8,128)} async-done(((f32[4096,16]{0,1:T(8,128)}), f32[512,16]{0,1:T(8,128)}) %reduce-scatter.7.cloned.1.call-update) | async-done | bytes 32784 | tf_op jit(solution)/shard_map/reduce_scatter | solution.py:67
  210.9 0.8 slice_subtract_fusion.1
  211.7 25.1 %all_gather.9 = f32[16,4096]{1,0:T(8,128)S(1)} all-gather(f32[16,512]{1,0:T(8,128)S(1)} %slice_subtract_fusion.1), channel_id=1, replica_groups=mesh['leaf'=4,'panel'=8] {'panel'}, dimensions={1}, use_global_device_ids=true | all-gather | bytes 294912 | tf_op jit(solution)/shard_map/all_gather | solution.py:79
  236.8 5.5 %fusion.64 = f32[16,512]{1,0:T(8,128)S(1)} fusion(f32[16,4096]{1,0:T(8,128)S(1)} %all_gather.9, bf16[512,4096]{1,0:T(8,128)(2,1)} %param.11), kind=kOutput, calls=%fused_computation.107 | convolution fusion | flops 402653184 | bytes 4489216 | tf_op jit(solution)/shard_map/dot_general | solution.py:78
  242.4 24.5 %all_gather.10 = f32[16,4096]{1,0:T(8,128)S(1)} all-gather(f32[16,512]{1,0:T(8,128)S(1)} %fusion.64), channel_id=1, replica_groups=mesh['leaf'=4,'panel'=8] {'panel'}, dimensions={1}, use_global_device_ids=true | all-gather | bytes 294912 | tf_op jit(solution)/shard_map/all_gather | solution.py:92
  266.8 3.9 fusion.31
  270.7 4.7 convolution_bitcast_fusion.2
  275.4 0.0 reduce-scatter.9.cloned.1.call-update
  275.4 0.0 reduce-scatter.11.cloned.1.call-start
  275.5 72.3 %reduce-scatter.9.cloned.1.call-done = f32[512,16]{0,1:T(8,128)} async-done(((f32[4096,16]{0,1:T(8,128)}), f32[512,16]{0,1:T(8,128)}) %reduce-scatter.9.cloned.1.call-update) | async-done | bytes 32784 | tf_op jit(solution)/shard_map/reduce_scatter | solution.py:98
  347.8 2.8 fusion.12
  350.6 1.2 collective-permute-start.8
  351.8 1.6 collective-permute-done.8
  353.4 0.1 copy.24
  353.6 25.7 %all_gather.11 = f32[32,4096]{1,0:T(8,128)S(1)} all-gather(f32[32,512]{1,0:T(8,128)S(1)} %select_n.142), channel_id=1, replica_groups=mesh['leaf'=4,'panel'=8] {'panel'}, dimensions={1}, use_global_device_ids=true | all-gather | bytes 589824 | tf_op jit(solution)/shard_map/all_gather | solution.py:92
  379.2 4.3 fusion.28
  383.5 0.0 copy-start
  383.5 5.2 %convolution_bitcast_fusion = f32[4096,32]{0,1:T(8,128)} fusion(f32[32,512]{1,0:T(8,128)S(1)} %fusion.28, bf16[2,1,512,4096]{3,2,1,0:T(8,128)(2,1)} %param.8), kind=kOutput, calls=%fused_computation | convolution fusion | flops 805306368 | bytes 4784128 | tf_op jit(solution)/shard_map/dot_general | solution.py:99
  388.7 0.0 reduce-scatter.11.cloned.1.call-update
  388.7 68.6 %reduce-scatter.11.cloned.1.call-done = f32[512,32]{0,1:T(8,128)} async-done(((f32[4096,32]{0,1:T(8,128)}), f32[512,32]{0,1:T(8,128)}) %reduce-scatter.11.cloned.1.call-update) | async-done | bytes 65552 | tf_op jit(solution)/shard_map/reduce_scatter | solution.py:98
  457.3 3.0 fusion.14
  460.4 2.6 collective-permute-start.9
  463.0 0.0 copy-done
  463.0 1.5 maximum_bitcast_fusion
  464.5 0.0 collective-permute-done.9
  464.5 0.1 copy.25
  464.6 0.7 select_n.148
  (30 shorter events, 0.3 us)
Async XLA Ops:
  7.2 105.5 %reduce-scatter.5.cloned.1.call-start = ((), (), s32[]{:S(2)}) async-start(), calls=%async_computation.4 | async-start | bytes 589824 | tf_op jit(solution)/shard_map/reduce_scatter | solution.py:67
  8.3 1.3 collective-permute-start
  12.2 6.8 %collective-permute-start.1 = (f32[32,512]{1,0:T(8,128)S(1)}, f32[32,512]{1,0:T(8,128)S(1)}, u32[]{:S(2)}, u32[]{:S(2)}) collective-permute-start(f32[32,512]{1,0:T(8,128)S(1)} %get-tuple-element.5), channel_id=1, source_target_pairs={{0,7},{1,0},{2,1},{3,2},{4,3},{5,4},{6,5},{7,6},{8,15},{9,8},{10,9... | collective-permute-start | bytes 196616 | tf_op jit(solution)/shard_map/ppermute | solution.py:16
  19.0 3.9 collective-permute-start.2
  22.9 14.5 %collective-permute-start.3 = (f32[32,2048]{1,0:T(8,128)S(1)}, f32[32,2048]{1,0:T(8,128)S(1)}, u32[]{:S(2)}, u32[]{:S(2)}) collective-permute-start(f32[32,2048]{1,0:T(8,128)S(1)} %pad_maximum_fusion), channel_id=1, source_target_pairs={{0,4},{1,5},{2,6},{3,7},{4,0},{5,1},{6,2},{7,3},{8,12},{9,13},{10,... | collective-permute-start | bytes 786440 | tf_op jit(solution)/shard_map/ppermute | solution.py:16
  50.0 160.9 %reduce-scatter.7.cloned.1.call-start = ((), (), s32[]{:S(2)}) async-start(), calls=%async_computation.5 | async-start | bytes 294912 | tf_op jit(solution)/shard_map/reduce_scatter | solution.py:67
  113.6 2.8 collective-permute-start.4
  118.7 3.3 collective-permute-start.5
  122.0 3.1 collective-permute-start.6
  125.1 6.6 %collective-permute-start.7 = (f32[16,2048]{1,0:T(8,128)S(1)}, f32[16,2048]{1,0:T(8,128)S(1)}, u32[]{:S(2)}, u32[]{:S(2)}) collective-permute-start(f32[16,2048]{1,0:T(8,128)S(1)} %pad_maximum_fusion.2), channel_id=1, source_target_pairs={{0,4},{1,5},{2,6},{3,7},{4,0},{5,1},{6,2},{7,3},{8,12},{9,13},{10,... | collective-permute-start | bytes 393224 | tf_op jit(solution)/shard_map/ppermute | solution.py:16
  143.6 204.2 %reduce-scatter.9.cloned.1.call-start = ((), (), s32[]{:S(2)}) async-start(), calls=%async_computation.6 | async-start | bytes 294912 | tf_op jit(solution)/shard_map/reduce_scatter | solution.py:98
  275.4 181.9 %reduce-scatter.11.cloned.1.call-start = ((), (), s32[]{:S(2)}) async-start(), calls=%async_computation.7 | async-start | bytes 589824 | tf_op jit(solution)/shard_map/reduce_scatter | solution.py:98
  350.6 2.8 collective-permute-start.8
  383.5 79.5 %copy-start = (f32[512,16]{0,1:T(8,128)S(1)}, f32[512,16]{0,1:T(8,128)}, u32[]{:S(2)}) copy-start(f32[512,16]{0,1:T(8,128)} %reduce-scatter.9.cloned.1.call-done) | copy-start | bytes 98308
  460.4 4.1 collective-permute-start.9
Sparse Core Ops, SparseCore 0:
  50.1 62.4 reduce-scatter.4
  143.7 67.1 reduce-scatter.6
  275.5 72.2 reduce-scatter.8
  388.8 68.4 reduce-scatter.10
